TPU v7x, 32 devices: a whole 2x2x4 slice. The times are simulated.
32 devices in a mesh: lon: 4 (over y, x), lat: 8 (over z, core).
Axes of the slice: x: 2, y: 2, z: 4, core: 2. Of those that a mesh axis runs over, the one named last changes fastest.
Arguments:
- state_adjoint: float32 [4, 4, 512, 1024], P(None, None, 'lat', 'lon'), may hold values from -6 to 6
- east_velocity: float32 [4, 512, 1024], P(None, 'lat', 'lon'), may hold values from -1.2 to 1.2
- north_velocity: float32 [4, 512, 1024], P(None, 'lat', 'lon'), may hold values from -1.2 to 1.2
- ocean_mask: int32 [4, 512, 1024], P(None, 'lat', 'lon'), may hold values 0 or 1
- partner: int32 [1024], P('lon'), may hold values from 0 to 1023, as said below
Outputs:
- sensitivity: float32 [4, 4, 512, 1024], P(None, None, 'lat', 'lon')
Inputs may be any that keep to these rules, and one draw needn't show every extreme that they name: partner[i] = (c - i) mod 1024 with one c for all columns, 1023 <= c <= 1278; hence partner[partner[i]] = i.
All inputs are finite; a program needn't handle non-finite values. No bound on the sum of `ocean_mask` on one device may be relied on, other than what follows from the above.
Results may differ from a plain program's by a relative error of at most 0.00002.
Values sent between devices are 32-bit elements; how exact they have to be, the bound alone decides.
No kernel may reach another device: no remote copies, remote signals or barrier semaphores. Data moves between devices by JAX's collectives and lax.ppermute only.
A program may use at most 64 MiB of HBM per device.

v0:
```python
import jax
import jax.numpy as jnp
from jax import lax
from jax.sharding import PartitionSpec as P

STEPS = 2


def shifted(shard, axis, by):
    count = lax.axis_size(axis)
    return lax.ppermute(shard, axis, [(i, (i + by) % count) for i in range(count)])


def shifted_2(shard, axis, by):
    count = lax.axis_size(axis)
    pairs = [(i, i + by) for i in range(count) if 0 <= i + by < count]
    return lax.ppermute(shard, axis, pairs)


def with_halo(block, sides, width, periodic):
    for axis, dim in sides:
        count = lax.axis_size(axis)
        forward = [(i, i + 1) for i in range(count - 1)]
        if periodic:
            forward.append((count - 1, 0))
        backward = [(target, source) for source, target in forward]
        low = lax.ppermute(
            lax.slice_in_dim(block, block.shape[dim] - width, None, axis=dim), axis, forward
        )
        high = lax.ppermute(lax.slice_in_dim(block, 0, width, axis=dim), axis, backward)
        block = jnp.concatenate([low, block, high], axis=dim)
    return block


def per_device(state_adjoint, east_velocity, north_velocity, ocean_mask, partner):
    wet_cells = ocean_mask.astype(jnp.float32)
    fold_signs = jnp.array([1.0, 1.0, -1.0, -1.0], dtype=jnp.float32).reshape(4, 1, 1)
    lat_place = lax.axis_index("lat")
    lat_count = lax.axis_size("lat")
    is_top = (lat_place == lat_count - 1).astype(jnp.float32)
    speed_west_edge = shifted(east_velocity[:, :, -1:], "lon", 1)
    speed_south_edge = shifted_2(north_velocity[:, -1:, :], "lat", 1)
    west_speed = jnp.concatenate([speed_west_edge, east_velocity[:, :, :-1]], axis=2)
    south_speed = jnp.concatenate([speed_south_edge, north_velocity[:, :-1, :]], axis=1)
    fold_weight = 1.0 + north_velocity[:, -1, :]
    current = state_adjoint
    for iteration in range(STEPS):
        masked = wet_cells * current
        lon_padded = with_halo(masked, (("lon", 3),), 1, True)
        lat_padded = with_halo(masked, (("lat", 2),), 1, False)
        west_rim = lon_padded[:, :, :, 0]
        east_rim = lon_padded[:, :, :, -1]
        south_rim = lat_padded[:, :, 0, :]
        north_rim = lat_padded[:, :, -1, :]
        east_adj = jnp.concatenate([masked[..., 1:], east_rim[..., None]], axis=3)
        west_adj = jnp.concatenate([west_rim[..., None], masked[..., :-1]], axis=3)
        north_adj = jnp.concatenate([masked[:, :, 1:, :], north_rim[:, :, None, :]], axis=2)
        south_adj = jnp.concatenate([south_rim[:, :, None, :], masked[:, :, :-1, :]], axis=2)
        transport = (
            0.5 * east_velocity * (east_adj - masked)
            + 0.5 * west_speed * (masked - west_adj)
            + 0.5 * north_velocity * (north_adj - masked)
            + 0.5 * south_speed * (masked - south_adj)
        )
        fold_flux = fold_weight * masked[:, :, -1, :]
        whole_row = lax.all_gather(fold_flux, "lon", axis=2, tiled=True)
        picked = jnp.take(whole_row, partner, axis=2)
        folded = 0.5 * fold_signs * picked
        total = masked + transport
        total = total.at[:, :, -1, :].add(is_top * folded)
        current = wet_cells * total
    return current


def solution(mesh):
    placed = (
        P(None, None, "lat", "lon"),
        P(None, "lat", "lon"),
        P(None, "lat", "lon"),
        P(None, "lat", "lon"),
        P("lon"),
    )
    return jax.shard_map(
        per_device,
        mesh=mesh,
        in_specs=placed,
        out_specs=P(None, None, "lat", "lon"),
        check_vma=False,
    )
```

profile of v0, /device:TPU:10, one launch (start us, length us, event | category | flops | bytes accessed | tf_op | source)
XLA Modules:
  0.0 109.1 jit_solution(16763126374377405692)
XLA Ops:
  0.8 1.9 %collective-permute-start.4 = (f32[4,1,256]{2,1,0:T(1,128)S(1)}, f32[4,1,256]{2,1,0:T(1,128)S(1)}, u32[]{:S(2)}, u32[]{:S(2)}) collective-permute-start(f32[4,1,256]{2,1,0:T(1,128)S(1)} %get-tuple-element.47), channel_id=1, source_target_pairs={{0,1},{1,2},{2,3},{3,4},{4,5},{5,6},{6,7},{8,9},{9,10},{10,11},{11... | collective-permute-start | bytes 12296 | tf_op jit(solution)/shard_map/ppermute | solution.py:17
  2.7 1.7 %slice.119 = f32[4,64,1]{2,1,0:T(8,128)} slice(f32[4,64,256]{2,1,0:T(8,128)} %param.13), slice={[0:4], [0:64], [255:256]} | slice | bytes 2048 | tf_op jit(solution)/shard_map/slice | solution.py:41
  4.3 1.5 %collective-permute-start.1 = (f32[4,64,1]{2,1,0:T(8,128)}, f32[4,64,1]{2,1,0:T(8,128)}, u32[]{:S(2)}, u32[]{:S(2)}) collective-permute-start(f32[4,64,1]{2,1,0:T(8,128)} %slice.119), channel_id=1, source_target_pairs={{0,8},{8,16},{16,24},{24,0},{1,9},{9,17},{17,25},{25,1},{2,10},{10... | collective-permute-start | bytes 3080 | tf_op jit(solution)/shard_map/ppermute | solution.py:11
  7.0 2.1 %copy_multiply_fusion = f32[4,4,64,256]{3,1,0,2:T(4,128)S(1)} fusion(f32[4,4,64,256]{3,2,1,0:T(8,128)} %param.12, f32[4,64,256]{2,0,1:T(4,128)S(1)} %copy.78), kind=kLoop, calls=%fused_computation.26 | loop fusion | flops 262144 | bytes 2359296 | tf_op jit(solution)/shard_map/mul | solution.py:48
  9.1 3.3 %collective-permute-start.5 = (f32[4,4,1,256]{3,1,0,2:T(4,128)S(1)}, f32[4,4,1,256]{3,1,0,2:T(4,128)S(1)}, u32[]{:S(2)}, u32[]{:S(2)}) collective-permute-start(f32[4,4,1,256]{3,1,0,2:T(4,128)S(1)} %get-tuple-element.38), channel_id=1, source_target_pairs={{0,1},{1,2},{2,3},{3,4},{4,5},{5,6},{6,7},{8,9},{9,10},{10,11},{11... | collective-permute-start | bytes 49160 | tf_op jit(solution)/shard_map/ppermute | solution.py:27
  12.4 2.3 %collective-permute-start.3 = (f32[4,4,1,256]{3,1,0,2:T(4,128)S(1)}, f32[4,4,1,256]{3,1,0,2:T(4,128)S(1)}, u32[]{:S(2)}, u32[]{:S(2)}) collective-permute-start(f32[4,4,1,256]{3,1,0,2:T(4,128)S(1)} %get-tuple-element.39), channel_id=1, source_target_pairs={{1,0},{2,1},{3,2},{4,3},{5,4},{6,5},{7,6},{9,8},{10,9},{11,10},{12... | collective-permute-start | bytes 49160 | tf_op jit(solution)/shard_map/ppermute | solution.py:30
  16.0 1.5 %collective-permute-start.2 = (f32[4,4,64,1]{3,1,0,2:T(4,128)}, f32[4,4,64,1]{3,1,0,2:T(4,128)}, u32[]{:S(2)}, u32[]{:S(2)}) collective-permute-start(f32[4,4,64,1]{3,1,0,2:T(4,128)} %get-tuple-element.42), channel_id=1, source_target_pairs={{0,8},{8,16},{16,24},{24,0},{1,9},{9,17},{17,25},{25,1},{2,10},{10... | collective-permute-start | bytes 12296 | tf_op jit(solution)/shard_map/ppermute | solution.py:27
  18.1 1.8 %fusion.25 = (f32[4,4,63,256]{3,1,0,2:T(4,128)}, f32[4,4,63,256]{3,1,0,2:T(4,128)}) fusion(f32[4,4,64,256]{3,1,0,2:T(4,128)S(1)} %copy_multiply_fusion), kind=kLoop, calls=%fused_computation.53 | loop fusion | bytes 4128768 | tf_op jit(solution)/shard_map/slice | solution.py:58
  19.9 1.7 %fusion.27 = (f32[4,4,64,255]{3,1,0,2:T(4,128)S(1)}, f32[4,4,64,255]{3,1,0,2:T(4,128)}) fusion(f32[4,4,64,256]{3,1,0,2:T(4,128)S(1)} %copy_multiply_fusion), kind=kLoop, calls=%fused_computation.55 | loop fusion | bytes 4177920 | tf_op jit(solution)/shard_map/slice | solution.py:56
  21.6 12.3 %all_gather.6 = f32[4,4,1024]{2,1,0:T(4,128)S(1)} all-gather(f32[4,4,256]{2,1,0:T(4,128)S(1)} %bitcast_multiply_fusion.3), channel_id=1, replica_groups=mesh['lon'=4,'lat'=8] {'lon'}, dimensions={2}, use_global_device_ids=true | all-gather | bytes 81920 | tf_op jit(solution)/shard_map/all_gather | solution.py:66
  35.7 1.7 %copy.84 = f32[4,4,1024]{1,0,2:T(4,128)} copy(f32[4,4,1024]{2,1,0:T(4,128)S(1)} %all_gather.6) | data formatting | bytes 131072 | tf_op jit(solution)/shard_map/all_gather | solution.py:66
  37.4 2.6 %gather_fusion = f32[256,4,4]{2,1,0:T(4,128)S(1)} fusion(f32[4,4,1024]{1,0,2:T(4,128)} %copy.84, s32[1024]{0:T(1024)S(1)} %pad_clamp_fusion), kind=kCustom, calls=%fused_computation.clone | custom fusion | bytes 33792 | tf_op jit(solution)/shard_map/jit(_take)/gather | solution.py:67
  42.1 12.2 %collective-permute-done = f32[4,4,64,1]{3,1,0,2:T(4,128)S(1)} collective-permute-done((f32[4,4,64,1]{3,1,0,2:T(4,128)}, f32[4,4,64,1]{3,1,0,2:T(4,128)S(1)}, u32[]{:S(2)}, u32[]{:S(2)}) %collective-permute-start) | collective-permute-done | bytes 4128 | tf_op jit(solution)/shard_map/ppermute | solution.py:30
  54.4 4.6 %fusion.4 = f32[4,4,64,256]{3,1,0,2:T(4,128)S(1)} fusion(f32[4,4,64,1]{3,1,0,2:T(4,128)S(1)} %collective-permute-done, f32[4,4,64,255]{3,1,0,2:T(4,128)} %get-tuple-element.45, f32[4,4,64,255]{3,1,0,2:T(4,128)S(1)} %get-tuple-element.44, f32[4,4,64,1]{3,1,0,2:T(4,128)} %collective-permute-done.2, f32[4,4,1,256]{3,1,0,2:T(4,128)S(1)} %collective-permute-done.3, ...), kind=kLoop, calls=%fused_computation.7 | loop fusion | flops 4456448 | bytes 7602176 | tf_op jit(solution)/shard_map/add | solution.py:69
  59.5 1.4 %fusion.22 = (f32[4,4,64,1]{3,1,0,2:T(4,128)}, f32[4,4,64,1]{3,1,0,2:T(4,128)}) fusion(f32[4,4,64,256]{3,1,0,2:T(4,128)S(1)} %multiply_multiply_fusion), kind=kLoop, calls=%fused_computation.50 | loop fusion | bytes 16384 | tf_op jit(solution)/shard_map/slice | solution.py:28
  60.8 1.8 %fusion.21 = (f32[4,4,63,256]{3,1,0,2:T(4,128)}, f32[4,4,63,256]{3,1,0,2:T(4,128)}) fusion(f32[4,4,64,256]{3,1,0,2:T(4,128)S(1)} %multiply_multiply_fusion), kind=kLoop, calls=%fused_computation.49 | loop fusion | bytes 4128768 | tf_op jit(solution)/shard_map/slice | solution.py:58
  63.4 1.9 %collective-permute-start.9 = (f32[4,4,1,256]{3,1,0,2:T(4,128)S(1)}, f32[4,4,1,256]{3,1,0,2:T(4,128)S(1)}, u32[]{:S(2)}, u32[]{:S(2)}) collective-permute-start(f32[4,4,1,256]{3,1,0,2:T(4,128)S(1)} %get-tuple-element.30), channel_id=1, source_target_pairs={{0,1},{1,2},{2,3},{3,4},{4,5},{5,6},{6,7},{8,9},{9,10},{10,11},{11... | collective-permute-start | bytes 49160 | tf_op jit(solution)/shard_map/ppermute | solution.py:27
  65.3 3.6 %collective-permute-start.8 = (f32[4,4,1,256]{3,1,0,2:T(4,128)S(1)}, f32[4,4,1,256]{3,1,0,2:T(4,128)S(1)}, u32[]{:S(2)}, u32[]{:S(2)}) collective-permute-start(f32[4,4,1,256]{3,1,0,2:T(4,128)S(1)} %get-tuple-element.31), channel_id=1, source_target_pairs={{1,0},{2,1},{3,2},{4,3},{5,4},{6,5},{7,6},{9,8},{10,9},{11,10},{12... | collective-permute-start | bytes 49160 | tf_op jit(solution)/shard_map/ppermute | solution.py:30
  69.4 1.7 %collective-permute-start.6 = (f32[4,4,64,1]{3,1,0,2:T(4,128)}, f32[4,4,64,1]{3,1,0,2:T(4,128)}, u32[]{:S(2)}, u32[]{:S(2)}) collective-permute-start(f32[4,4,64,1]{3,1,0,2:T(4,128)} %get-tuple-element.35), channel_id=1, source_target_pairs={{8,0},{16,8},{24,16},{0,24},{9,1},{17,9},{25,17},{1,25},{10,2},{18... | collective-permute-start | bytes 12296 | tf_op jit(solution)/shard_map/ppermute | solution.py:30
  71.0 25.6 %all_gather.7 = f32[4,4,1024]{2,1,0:T(4,128)S(1)} all-gather(f32[4,4,256]{2,1,0:T(4,128)S(1)} %bitcast_multiply_fusion.1), channel_id=1, replica_groups=mesh['lon'=4,'lat'=8] {'lon'}, dimensions={2}, use_global_device_ids=true | all-gather | bytes 81920 | tf_op jit(solution)/shard_map/all_gather | solution.py:66
  96.7 1.7 %copy.86 = f32[4,4,1024]{1,0,2:T(4,128)} copy(f32[4,4,1024]{2,1,0:T(4,128)S(1)} %all_gather.7) | data formatting | bytes 131072 | tf_op jit(solution)/shard_map/all_gather | solution.py:66
  98.4 3.4 %gather_fusion.1 = f32[256,4,4]{2,1,0:T(4,128)} fusion(f32[4,4,1024]{1,0,2:T(4,128)} %copy.86, s32[1024]{0:T(1024)S(1)} %pad_clamp_fusion), kind=kCustom, calls=%fused_computation.1.clone | custom fusion | bytes 33792 | tf_op jit(solution)/shard_map/jit(_take)/gather | solution.py:67
  103.0 4.1 %fusion.12 = f32[4,4,64,256]{3,1,0,2:T(4,128)S(1)} fusion(f32[4,4,64,1]{3,1,0,2:T(4,128)} %collective-permute-done.6, f32[4,4,64,255]{3,1,0,2:T(4,128)S(1)} %get-tuple-element.37, f32[4,4,64,255]{3,1,0,2:T(4,128)S(1)} %get-tuple-element.36, f32[4,4,64,1]{3,1,0,2:T(4,128)} %collective-permute-done.7, f32[4,4,1,256]{3,1,0,2:T(4,128)S(1)} %collective-permute-done.8, ...), kind=kLoop, calls=%fused_computation.19 | loop fusion | flops 4718592 | bytes 7602176 | tf_op jit(solution)/shard_map/add | solution.py:69
  107.5 1.6 %copy.88 = f32[4,4,64,256]{3,2,1,0:T(8,128)} copy(f32[4,4,64,256]{3,1,0,2:T(4,128)S(1)} %broadcast_multiply_fusion) | data formatting | bytes 2097152 | tf_op jit(solution)/shard_map/mul | solution.py:71
  (56 shorter events, 10.8 us)
Async XLA Ops:
  0.8 41.1 %collective-permute-start.4 = (f32[4,1,256]{2,1,0:T(1,128)S(1)}, f32[4,1,256]{2,1,0:T(1,128)S(1)}, u32[]{:S(2)}, u32[]{:S(2)}) collective-permute-start(f32[4,1,256]{2,1,0:T(1,128)S(1)} %get-tuple-element.47), channel_id=1, source_target_pairs={{0,1},{1,2},{2,3},{3,4},{4,5},{5,6},{6,7},{8,9},{9,10},{10,11},{11... | collective-permute-start | bytes 12296 | tf_op jit(solution)/shard_map/ppermute | solution.py:17
  4.3 35.8 %collective-permute-start.1 = (f32[4,64,1]{2,1,0:T(8,128)}, f32[4,64,1]{2,1,0:T(8,128)}, u32[]{:S(2)}, u32[]{:S(2)}) collective-permute-start(f32[4,64,1]{2,1,0:T(8,128)} %slice.119), channel_id=1, source_target_pairs={{0,8},{8,16},{16,24},{24,0},{1,9},{9,17},{17,25},{25,1},{2,10},{10... | collective-permute-start | bytes 3080 | tf_op jit(solution)/shard_map/ppermute | solution.py:11
  7.0 10.5 %copy-start.8 = (s32[256]{0:T(256)S(1)}, s32[256]{0:T(256)}, u32[]{:S(2)}) copy-start(s32[256]{0:T(256)} %param.16) | copy-start | bytes 3076
  7.0 11.0 %copy-start.4 = (f32[4,64,256]{2,1,0:T(8,128)S(1)}, f32[4,64,256]{2,1,0:T(8,128)}, u32[]{:S(2)}) copy-start(f32[4,64,256]{2,1,0:T(8,128)} %param.13) | copy-start | bytes 786436
  7.0 11.0 %copy-start.5 = (f32[4,64,256]{2,1,0:T(8,128)S(1)}, f32[4,64,256]{2,1,0:T(8,128)}, u32[]{:S(2)}) copy-start(f32[4,64,256]{2,1,0:T(8,128)} %param.14) | copy-start | bytes 786436
  9.1 45.2 %collective-permute-start.5 = (f32[4,4,1,256]{3,1,0,2:T(4,128)S(1)}, f32[4,4,1,256]{3,1,0,2:T(4,128)S(1)}, u32[]{:S(2)}, u32[]{:S(2)}) collective-permute-start(f32[4,4,1,256]{3,1,0,2:T(4,128)S(1)} %get-tuple-element.38), channel_id=1, source_target_pairs={{0,1},{1,2},{2,3},{3,4},{4,5},{5,6},{6,7},{8,9},{9,10},{10,11},{11... | collective-permute-start | bytes 49160 | tf_op jit(solution)/shard_map/ppermute | solution.py:27
  12.4 41.9 %collective-permute-start.3 = (f32[4,4,1,256]{3,1,0,2:T(4,128)S(1)}, f32[4,4,1,256]{3,1,0,2:T(4,128)S(1)}, u32[]{:S(2)}, u32[]{:S(2)}) collective-permute-start(f32[4,4,1,256]{3,1,0,2:T(4,128)S(1)} %get-tuple-element.39), channel_id=1, source_target_pairs={{1,0},{2,1},{3,2},{4,3},{5,4},{6,5},{7,6},{9,8},{10,9},{11,10},{12... | collective-permute-start | bytes 49160 | tf_op jit(solution)/shard_map/ppermute | solution.py:30
  16.0 26.0 %collective-permute-start.2 = (f32[4,4,64,1]{3,1,0,2:T(4,128)}, f32[4,4,64,1]{3,1,0,2:T(4,128)}, u32[]{:S(2)}, u32[]{:S(2)}) collective-permute-start(f32[4,4,64,1]{3,1,0,2:T(4,128)} %get-tuple-element.42), channel_id=1, source_target_pairs={{0,8},{8,16},{16,24},{24,0},{1,9},{9,17},{17,25},{25,1},{2,10},{10... | collective-permute-start | bytes 12296 | tf_op jit(solution)/shard_map/ppermute | solution.py:27
  35.7 18.7 %copy-start = (f32[4,4,64,256]{3,2,1,0:T(8,128)S(1)}, f32[4,4,64,256]{3,2,1,0:T(8,128)}, u32[]{:S(2)}) copy-start(f32[4,4,64,256]{3,2,1,0:T(8,128)} %param.12) | copy-start | bytes 3145732
  40.2 14.2 %copy-start.1 = (f32[4,64,256]{2,0,1:T(4,128)S(1)}, f32[4,64,256]{2,0,1:T(4,128)}, u32[]{:S(2)}) copy-start(f32[4,64,256]{2,0,1:T(4,128)} %copy.82) | copy-start | bytes 786436
  40.2 14.1 %collective-permute-start = (f32[4,4,64,1]{3,1,0,2:T(4,128)}, f32[4,4,64,1]{3,1,0,2:T(4,128)S(1)}, u32[]{:S(2)}, u32[]{:S(2)}) collective-permute-start(f32[4,4,64,1]{3,1,0,2:T(4,128)} %get-tuple-element.43), channel_id=1, source_target_pairs={{8,0},{16,8},{24,16},{0,24},{9,1},{17,9},{25,17},{1,25},{10,2},{18... | collective-permute-start | bytes 12296 | tf_op jit(solution)/shard_map/ppermute | solution.py:30
  41.8 17.2 %copy-start.2 = (f32[4,64,256]{2,0,1:T(4,128)}, f32[4,64,256]{2,0,1:T(4,128)S(1)}, u32[]{:S(2)}) copy-start(f32[4,64,256]{2,0,1:T(4,128)S(1)} %copy.81) | copy-start | bytes 786436
  42.1 17.0 %copy-start.3 = (f32[4,64,256]{2,0,1:T(4,128)}, f32[4,64,256]{2,0,1:T(4,128)S(1)}, u32[]{:S(2)}) copy-start(f32[4,64,256]{2,0,1:T(4,128)S(1)} %copy.83) | copy-start | bytes 786436
  54.3 4.7 %copy-start.6 = (f32[4]{0:T(128)S(1)}, f32[4]{0:T(128)}, u32[]{:S(2)}) copy-start(f32[4]{0:T(128)} %constant.73) | copy-start | bytes 52
  54.4 4.7 %copy-start.7 = (pred[256]{0:T(512)(128)(4,1)S(1)}, pred[256]{0:T(512)(128)(4,1)}, u32[]{:S(2)}) copy-start(pred[256]{0:T(512)(128)(4,1)} %compare_and_fusion) | copy-start | bytes 772
  63.4 39.6 %collective-permute-start.9 = (f32[4,4,1,256]{3,1,0,2:T(4,128)S(1)}, f32[4,4,1,256]{3,1,0,2:T(4,128)S(1)}, u32[]{:S(2)}, u32[]{:S(2)}) collective-permute-start(f32[4,4,1,256]{3,1,0,2:T(4,128)S(1)} %get-tuple-element.30), channel_id=1, source_target_pairs={{0,1},{1,2},{2,3},{3,4},{4,5},{5,6},{6,7},{8,9},{9,10},{10,11},{11... | collective-permute-start | bytes 49160 | tf_op jit(solution)/shard_map/ppermute | solution.py:27
  65.3 37.7 %collective-permute-start.8 = (f32[4,4,1,256]{3,1,0,2:T(4,128)S(1)}, f32[4,4,1,256]{3,1,0,2:T(4,128)S(1)}, u32[]{:S(2)}, u32[]{:S(2)}) collective-permute-start(f32[4,4,1,256]{3,1,0,2:T(4,128)S(1)} %get-tuple-element.31), channel_id=1, source_target_pairs={{1,0},{2,1},{3,2},{4,3},{5,4},{6,5},{7,6},{9,8},{10,9},{11,10},{12... | collective-permute-start | bytes 49160 | tf_op jit(solution)/shard_map/ppermute | solution.py:30
  69.0 34.0 %collective-permute-start.7 = (f32[4,4,64,1]{3,1,0,2:T(4,128)}, f32[4,4,64,1]{3,1,0,2:T(4,128)}, u32[]{:S(2)}, u32[]{:S(2)}) collective-permute-start(f32[4,4,64,1]{3,1,0,2:T(4,128)} %get-tuple-element.34), channel_id=1, source_target_pairs={{0,8},{8,16},{16,24},{24,0},{1,9},{9,17},{17,25},{25,1},{2,10},{10... | collective-permute-start | bytes 12296 | tf_op jit(solution)/shard_map/ppermute | solution.py:27
  69.4 33.6 %collective-permute-start.6 = (f32[4,4,64,1]{3,1,0,2:T(4,128)}, f32[4,4,64,1]{3,1,0,2:T(4,128)}, u32[]{:S(2)}, u32[]{:S(2)}) collective-permute-start(f32[4,4,64,1]{3,1,0,2:T(4,128)} %get-tuple-element.35), channel_id=1, source_target_pairs={{8,0},{16,8},{24,16},{0,24},{9,1},{17,9},{25,17},{1,25},{10,2},{18... | collective-permute-start | bytes 12296 | tf_op jit(solution)/shard_map/ppermute | solution.py:30
where the time goes:
time: 110 us; the launch traced here: 109 us
  blocking collectives  37.9 us (34%)
  local copies, waits for them, and re-layouts  25.1 us (23%)
  starting transfers between devices  18.5 us (17%)
  other arithmetic  14.9 us (14%)
  waiting for transfers between devices  12.3 us (11%)
    all_gather x2, blocking collectives, per_device(): whole_row = lax.all_gather(fold_flux, 'lon', axis=2, tiled=True)  37.9 us
    ppermute x4, waiting for transfers between devices, with_halo(): lax.ppermute(lax.slice_in_dim(block, 0, width, axis=dim), axis, backward)  12.2 us
    add x2, other arithmetic, per_device(): total = masked + transport  8.75 us
    ppermute x4, starting transfers between devices, with_halo(): lax.ppermute(lax.slice_in_dim(block, 0, width, axis=dim), axis, backward)  8 us
    gather x4, local copies, waits for them, and re-layouts, per_device(): picked = jnp.take(whole_row, partner, axis=2)  7.4 us
    ppermute x4, starting transfers between devices, with_halo(): lax.ppermute(lax.slice_in_dim(block, block.shape[dim] - width, None, axis...  7.11 us
    slice x2, local copies, waits for them, and re-layouts, per_device(): masked[:, :, :-1, :]  3.65 us
    all_gather x2, local copies, waits for them, and re-layouts, per_device(): whole_row = lax.all_gather(fold_flux, 'lon', axis=2, tiled=True)  3.41 us
  transfers between devices with their start and end apart: 10, of which 1 were waited for; matrix products, arithmetic and copies ran while one was open for 22% of the time, Pallas kernels for 0%

commit v1 on v0

--- a/solution.py
+++ b/solution.py
@@ -63,7 +63,14 @@
             + 0.5 * south_speed * (masked - south_adj)
         )
         fold_flux = fold_weight * masked[:, :, -1, :]
-        whole_row = lax.all_gather(fold_flux, "lon", axis=2, tiled=True)
+        ring = [fold_flux]
+        for hop in range(3):
+            ring.append(lax.ppermute(ring[-1], "lon", [(dev, (dev + 1) % 4) for dev in range(4)]))
+        whole_row = jnp.roll(
+            jnp.concatenate(ring[::-1], axis=2),
+            (lax.axis_index("lon") + 1) * ring[0].shape[2],
+            axis=2,
+        )
         picked = jnp.take(whole_row, partner, axis=2)
         folded = 0.5 * fold_signs * picked
         total = masked + transport

time: 110 us -> 109 us (level)
  blocking collectives: 37.9 us -> 0 us
  waiting for transfers between devices: 12.3 us -> 40.7 us
  starting transfers between devices: 18.5 us -> 30.4 us
  local copies, waits for them, and re-layouts: 25.1 us -> 20.1 us
  other arithmetic: 14.9 us -> 16.6 us
    ppermute x0 -> x6, waiting for transfers between devices: none -> 40.7 us  [per_device(): lax.ppermute(ring[-1], 'lon', [(dev, (dev + 1) % 4) for dev in range(4)])]
    all_gather x2 -> x0, blocking collectives: 37.9 us -> none  [per_device(): whole_row = lax.all_gather(fold_flux, 'lon', axis=2, tiled=True)]
    ppermute x4, waiting for transfers between devices: 12.2 us -> 0.01 us  [with_halo(): lax.ppermute(lax.slice_in_dim(block, 0, width, axis=dim), axis, backward)]
    ppermute x0 -> x6, starting transfers between devices: none -> 11.2 us  [per_device(): lax.ppermute(ring[-1], 'lon', [(dev, (dev + 1) % 4) for dev in range(4)])]
    all_gather x2 -> x0, local copies, waits for them, and re-layouts: 3.41 us -> none  [per_device(): whole_row = lax.all_gather(fold_flux, 'lon', axis=2, tiled=True)]
    unnamed x19 -> x39, local copies, waits for them, and re-layouts: 0.05 us -> 1.85 us
    add x2, other arithmetic: 8.75 us -> 7.08 us  [per_device(): total = masked + transport]
    slice x2, local copies, waits for them, and re-layouts: 3.65 us -> 2.14 us  [per_device(): masked[:, :, :-1, :]]
  transfers between devices with their start and end apart: 10 -> 16, of which waited for: 1 -> 2; matrix products, arithmetic and copies ran while one was open for 22% -> 21% of each run, Pallas kernels for 0% -> 0%
where the time goes in v1:
time: 109 us; the launch traced here: 108 us
  waiting for transfers between devices  40.7 us (37%)
  starting transfers between devices  30.4 us (28%)
  local copies, waits for them, and re-layouts  20.1 us (18%)
  other arithmetic  16.6 us (15%)
    ppermute x6, waiting for transfers between devices, per_device(): lax.ppermute(ring[-1], 'lon', [(dev, (dev + 1) % 4) for dev in range(4)])  40.7 us
    ppermute x6, starting transfers between devices, per_device(): lax.ppermute(ring[-1], 'lon', [(dev, (dev + 1) % 4) for dev in range(4)])  11.2 us
    ppermute x4, starting transfers between devices, with_halo(): lax.ppermute(lax.slice_in_dim(block, block.shape[dim] - width, None, axis...  7.9 us
    ppermute x4, starting transfers between devices, with_halo(): lax.ppermute(lax.slice_in_dim(block, 0, width, axis=dim), axis, backward)  7.78 us
    add x2, other arithmetic, per_device(): total = masked + transport  7.08 us
    gather x4, local copies, waits for them, and re-layouts, per_device(): picked = jnp.take(whole_row, partner, axis=2)  5.96 us
    slice x2, local copies, waits for them, and re-layouts, per_device(): west_adj = jnp.concatenate([west_rim[..., None], masked[..., :-1]], axis=3)  2.4 us
    mul x2, other arithmetic, per_device(): masked = wet_cells * current  2.31 us
  transfers between devices with their start and end apart: 16, of which 2 were waited for; matrix products, arithmetic and copies ran while one was open for 21% of the time, Pallas kernels for 0%

profile of v1, /device:TPU:10, one launch (start us, length us, event | category | flops | bytes accessed | tf_op | source)
XLA Modules:
  0.0 108.2 jit_solution(12728100343864229655)
XLA Ops:
  0.0 1.4 %broadcast_add_fusion = (f32[4,1,256]{2,1,0:T(1,128)S(1)}, f32[4,1,256]{2,1,0:T(1,128)}) fusion(f32[4,64,256]{2,1,0:T(8,128)} %param.16), kind=kLoop, calls=%fused_computation.76 | loop fusion | flops 1024 | bytes 12288 | tf_op jit(solution)/shard_map/add | solution.py:45
  1.4 2.0 %collective-permute-start.4 = (f32[4,1,256]{2,1,0:T(1,128)}, f32[4,1,256]{2,1,0:T(1,128)}, u32[]{:S(2)}, u32[]{:S(2)}) collective-permute-start(f32[4,1,256]{2,1,0:T(1,128)} %get-tuple-element.48), channel_id=1, source_target_pairs={{0,1},{1,2},{2,3},{3,4},{4,5},{5,6},{6,7},{8,9},{9,10},{10,11},{11... | collective-permute-start | bytes 12296 | tf_op jit(solution)/shard_map/ppermute | solution.py:17
  3.5 1.7 %slice.119 = f32[4,64,1]{2,1,0:T(8,128)} slice(f32[4,64,256]{2,1,0:T(8,128)} %param.15), slice={[0:4], [0:64], [255:256]} | slice | bytes 2048 | tf_op jit(solution)/shard_map/slice | solution.py:41
  5.1 1.5 %collective-permute-start.1 = (f32[4,64,1]{2,1,0:T(8,128)}, f32[4,64,1]{2,1,0:T(8,128)S(1)}, u32[]{:S(2)}, u32[]{:S(2)}) collective-permute-start(f32[4,64,1]{2,1,0:T(8,128)} %slice.119), channel_id=1, source_target_pairs={{0,8},{8,16},{16,24},{24,0},{1,9},{9,17},{17,25},{25,1},{2,10},{10... | collective-permute-start | bytes 3080 | tf_op jit(solution)/shard_map/ppermute | solution.py:11
  7.8 2.0 %copy_multiply_fusion = f32[4,4,64,256]{3,1,0,2:T(4,128)S(1)} fusion(f32[4,4,64,256]{3,2,1,0:T(8,128)} %param.14, f32[4,64,256]{2,0,1:T(4,128)S(1)} %copy.90), kind=kLoop, calls=%fused_computation.26 | loop fusion | flops 262144 | bytes 2359296 | tf_op jit(solution)/shard_map/mul | solution.py:48
  9.8 1.5 %collective-permute-start.6 = (f32[4,4,256]{2,1,0:T(4,128)S(1)}, f32[4,4,256]{2,1,0:T(4,128)}, u32[]{:S(2)}, u32[]{:S(2)}) collective-permute-start(f32[4,4,256]{2,1,0:T(4,128)S(1)} %bitcast_multiply_fusion.3), channel_id=1, source_target_pairs={{0,8},{8,16},{16,24},{24,0},{1,9},{9,17},{17,25},{25,1},{2,10},{10... | collective-permute-start | bytes 49160 | tf_op jit(solution)/shard_map/ppermute | solution.py:68
  12.0 3.0 %collective-permute-start.5 = (f32[4,4,1,256]{3,1,0,2:T(4,128)}, f32[4,4,1,256]{3,1,0,2:T(4,128)}, u32[]{:S(2)}, u32[]{:S(2)}) collective-permute-start(f32[4,4,1,256]{3,1,0,2:T(4,128)} %get-tuple-element.39), channel_id=1, source_target_pairs={{0,1},{1,2},{2,3},{3,4},{4,5},{5,6},{6,7},{8,9},{9,10},{10,11},{11... | collective-permute-start | bytes 49160 | tf_op jit(solution)/shard_map/ppermute | solution.py:27
  15.0 2.5 %collective-permute-start.3 = (f32[4,4,1,256]{3,1,0,2:T(4,128)}, f32[4,4,1,256]{3,1,0,2:T(4,128)}, u32[]{:S(2)}, u32[]{:S(2)}) collective-permute-start(f32[4,4,1,256]{3,1,0,2:T(4,128)} %get-tuple-element.40), channel_id=1, source_target_pairs={{1,0},{2,1},{3,2},{4,3},{5,4},{6,5},{7,6},{9,8},{10,9},{11,10},{12... | collective-permute-start | bytes 49160 | tf_op jit(solution)/shard_map/ppermute | solution.py:30
  20.1 1.9 %fusion.39 = (f32[4,4,63,256]{3,1,0,2:T(4,128)}, f32[4,4,63,256]{3,1,0,2:T(4,128)}) fusion(f32[4,4,64,256]{3,1,0,2:T(4,128)S(1)} %copy_multiply_fusion), kind=kLoop, calls=%fused_computation.83 | loop fusion | bytes 4128768 | tf_op jit(solution)/shard_map/slice | solution.py:58
  21.9 1.7 %fusion.41 = (f32[4,4,64,255]{3,1,0,2:T(4,128)S(1)}, f32[4,4,64,255]{3,1,0,2:T(4,128)}) fusion(f32[4,4,64,256]{3,1,0,2:T(4,128)S(1)} %copy_multiply_fusion), kind=kLoop, calls=%fused_computation.85 | loop fusion | bytes 4177920 | tf_op jit(solution)/shard_map/slice | solution.py:56
  27.6 1.6 %collective-permute-start = (f32[4,4,64,1]{3,1,0,2:T(4,128)}, f32[4,4,64,1]{3,1,0,2:T(4,128)S(1)}, u32[]{:S(2)}, u32[]{:S(2)}) collective-permute-start(f32[4,4,64,1]{3,1,0,2:T(4,128)} %get-tuple-element.44), channel_id=1, source_target_pairs={{8,0},{16,8},{24,16},{0,24},{9,1},{17,9},{25,17},{1,25},{10,2},{18... | collective-permute-start | bytes 12296 | tf_op jit(solution)/shard_map/ppermute | solution.py:30
  29.2 1.4 %collective-permute-start.7 = (f32[4,4,256]{2,1,0:T(4,128)}, f32[4,4,256]{2,1,0:T(4,128)S(1)}, u32[]{:S(2)}, u32[]{:S(2)}) collective-permute-start(f32[4,4,256]{2,1,0:T(4,128)} %collective-permute-done.6), channel_id=1, source_target_pairs={{0,8},{8,16},{16,24},{24,0},{1,9},{9,17},{17,25},{25,1},{2,10},{10... | collective-permute-start | bytes 49160 | tf_op jit(solution)/shard_map/ppermute | solution.py:68
  31.5 20.9 %collective-permute-done.7 = f32[4,4,256]{2,1,0:T(4,128)S(1)} collective-permute-done((f32[4,4,256]{2,1,0:T(4,128)}, f32[4,4,256]{2,1,0:T(4,128)S(1)}, u32[]{:S(2)}, u32[]{:S(2)}) %collective-permute-start.7) | collective-permute-done | bytes 16416 | tf_op jit(solution)/shard_map/ppermute | solution.py:68
  53.8 4.3 %fusion.4 = f32[4,4,64,256]{3,1,0,2:T(4,128)S(1)} fusion(f32[4,4,64,1]{3,1,0,2:T(4,128)S(1)} %collective-permute-done, f32[4,4,64,255]{3,1,0,2:T(4,128)S(1)} %copy-done.1, f32[4,4,64,255]{3,1,0,2:T(4,128)S(1)} %get-tuple-element.45, f32[4,4,64,1]{3,1,0,2:T(4,128)S(1)} %collective-permute-done.2, f32[4,4,1,256]{3,1,0,2:T(4,128)} %collective-permute-done.3, ...), kind=kLoop, calls=%fused_computation.7 | loop fusion | flops 4456448 | bytes 7602176 | tf_op jit(solution)/shard_map/add | solution.py:76
  60.0 1.8 %gather_fusion = f32[256,4,4]{2,1,0:T(4,128)} fusion(f32[4,4,1024]{1,0,2:T(4,128)S(1)} %copy.102, s32[1024]{0:T(1024)S(1)} %copy-done.14), kind=kCustom, calls=%fused_computation.clone | custom fusion | bytes 33792 | tf_op jit(solution)/shard_map/jit(_take)/gather | solution.py:74
  65.1 1.9 %collective-permute-start.12 = (f32[4,4,1,256]{3,1,0,2:T(4,128)S(1)}, f32[4,4,1,256]{3,1,0,2:T(4,128)S(1)}, u32[]{:S(2)}, u32[]{:S(2)}) collective-permute-start(f32[4,4,1,256]{3,1,0,2:T(4,128)S(1)} %get-tuple-element.31), channel_id=1, source_target_pairs={{0,1},{1,2},{2,3},{3,4},{4,5},{5,6},{6,7},{8,9},{9,10},{10,11},{11... | collective-permute-start | bytes 49160 | tf_op jit(solution)/shard_map/ppermute | solution.py:27
  67.0 3.6 %collective-permute-start.11 = (f32[4,4,1,256]{3,1,0,2:T(4,128)S(1)}, f32[4,4,1,256]{3,1,0,2:T(4,128)S(1)}, u32[]{:S(2)}, u32[]{:S(2)}) collective-permute-start(f32[4,4,1,256]{3,1,0,2:T(4,128)S(1)} %get-tuple-element.32), channel_id=1, source_target_pairs={{1,0},{2,1},{3,2},{4,3},{5,4},{6,5},{7,6},{9,8},{10,9},{11,10},{12... | collective-permute-start | bytes 49160 | tf_op jit(solution)/shard_map/ppermute | solution.py:30
  70.7 2.4 %collective-permute-start.10 = (f32[4,4,64,1]{3,1,0,2:T(4,128)S(1)}, f32[4,4,64,1]{3,1,0,2:T(4,128)S(1)}, u32[]{:S(2)}, u32[]{:S(2)}) collective-permute-start(f32[4,4,64,1]{3,1,0,2:T(4,128)S(1)} %get-tuple-element.35), channel_id=1, source_target_pairs={{0,8},{8,16},{16,24},{24,0},{1,9},{9,17},{17,25},{25,1},{2,10},{10... | collective-permute-start | bytes 12296 | tf_op jit(solution)/shard_map/ppermute | solution.py:27
  73.1 2.9 %collective-permute-start.14 = (f32[4,4,256]{2,1,0:T(4,128)S(1)}, f32[4,4,256]{2,1,0:T(4,128)S(1)}, u32[]{:S(2)}, u32[]{:S(2)}) collective-permute-start(f32[4,4,256]{2,1,0:T(4,128)S(1)} %collective-permute-done.13), channel_id=1, source_target_pairs={{0,8},{8,16},{16,24},{24,0},{1,9},{9,17},{17,25},{25,1},{2,10},{10... | collective-permute-start | bytes 49160 | tf_op jit(solution)/shard_map/ppermute | solution.py:68
  76.3 19.8 %collective-permute-done.14 = f32[4,4,256]{2,1,0:T(4,128)S(1)} collective-permute-done((f32[4,4,256]{2,1,0:T(4,128)S(1)}, f32[4,4,256]{2,1,0:T(4,128)S(1)}, u32[]{:S(2)}, u32[]{:S(2)}) %collective-permute-start.14) | collective-permute-done | bytes 16416 | tf_op jit(solution)/shard_map/ppermute | solution.py:68
  96.1 3.3 %collective-permute-start.15 = (f32[4,4,256]{2,1,0:T(4,128)S(1)}, f32[4,4,256]{2,1,0:T(4,128)S(1)}, u32[]{:S(2)}, u32[]{:S(2)}) collective-permute-start(f32[4,4,256]{2,1,0:T(4,128)S(1)} %collective-permute-done.14), channel_id=1, source_target_pairs={{0,8},{8,16},{16,24},{24,0},{1,9},{9,17},{17,25},{25,1},{2,10},{10... | collective-permute-start | bytes 49160 | tf_op jit(solution)/shard_map/ppermute | solution.py:68
  99.5 2.7 %fusion.12 = f32[4,4,64,256]{3,1,0,2:T(4,128)S(1)} fusion(f32[4,4,64,1]{3,1,0,2:T(4,128)S(1)} %collective-permute-done.9, f32[4,4,64,255]{3,1,0,2:T(4,128)S(1)} %get-tuple-element.38, f32[4,4,64,255]{3,1,0,2:T(4,128)S(1)} %get-tuple-element.37, f32[4,4,64,1]{3,1,0,2:T(4,128)S(1)} %collective-permute-done.10, ...), kind=kLoop, calls=%fused_computation.19 | loop fusion | flops 4718592 | bytes 7602176 | tf_op jit(solution)/shard_map/add | solution.py:76
  103.3 1.8 %gather_fusion.1 = f32[256,4,4]{2,1,0:T(4,128)} fusion(f32[4,4,1024]{1,0,2:T(4,128)S(1)} %copy.103, s32[1024]{0:T(1024)S(1)} %copy-done.14), kind=kCustom, calls=%fused_computation.1.clone | custom fusion | bytes 33792 | tf_op jit(solution)/shard_map/jit(_take)/gather | solution.py:74
  106.6 1.6 %copy.100 = f32[4,4,64,256]{3,2,1,0:T(8,128)} copy(f32[4,4,64,256]{3,1,0,2:T(4,128)S(1)} %broadcast_multiply_fusion) | data formatting | bytes 2097152 | tf_op jit(solution)/shard_map/mul | solution.py:78
  (86 shorter events, 18.5 us)
Async XLA Ops:
  1.4 26.2 %collective-permute-start.4 = (f32[4,1,256]{2,1,0:T(1,128)}, f32[4,1,256]{2,1,0:T(1,128)}, u32[]{:S(2)}, u32[]{:S(2)}) collective-permute-start(f32[4,1,256]{2,1,0:T(1,128)} %get-tuple-element.48), channel_id=1, source_target_pairs={{0,1},{1,2},{2,3},{3,4},{4,5},{5,6},{6,7},{8,9},{9,10},{10,11},{11... | collective-permute-start | bytes 12296 | tf_op jit(solution)/shard_map/ppermute | solution.py:17
  5.1 21.6 %collective-permute-start.1 = (f32[4,64,1]{2,1,0:T(8,128)}, f32[4,64,1]{2,1,0:T(8,128)S(1)}, u32[]{:S(2)}, u32[]{:S(2)}) collective-permute-start(f32[4,64,1]{2,1,0:T(8,128)} %slice.119), channel_id=1, source_target_pairs={{0,8},{8,16},{16,24},{24,0},{1,9},{9,17},{17,25},{25,1},{2,10},{10... | collective-permute-start | bytes 3080 | tf_op jit(solution)/shard_map/ppermute | solution.py:11
  9.8 19.4 %collective-permute-start.6 = (f32[4,4,256]{2,1,0:T(4,128)S(1)}, f32[4,4,256]{2,1,0:T(4,128)}, u32[]{:S(2)}, u32[]{:S(2)}) collective-permute-start(f32[4,4,256]{2,1,0:T(4,128)S(1)} %bitcast_multiply_fusion.3), channel_id=1, source_target_pairs={{0,8},{8,16},{16,24},{24,0},{1,9},{9,17},{17,25},{25,1},{2,10},{10... | collective-permute-start | bytes 49160 | tf_op jit(solution)/shard_map/ppermute | solution.py:68
  12.0 41.8 %collective-permute-start.5 = (f32[4,4,1,256]{3,1,0,2:T(4,128)}, f32[4,4,1,256]{3,1,0,2:T(4,128)}, u32[]{:S(2)}, u32[]{:S(2)}) collective-permute-start(f32[4,4,1,256]{3,1,0,2:T(4,128)} %get-tuple-element.39), channel_id=1, source_target_pairs={{0,1},{1,2},{2,3},{3,4},{4,5},{5,6},{6,7},{8,9},{9,10},{10,11},{11... | collective-permute-start | bytes 49160 | tf_op jit(solution)/shard_map/ppermute | solution.py:27
  15.0 38.8 %collective-permute-start.3 = (f32[4,4,1,256]{3,1,0,2:T(4,128)}, f32[4,4,1,256]{3,1,0,2:T(4,128)}, u32[]{:S(2)}, u32[]{:S(2)}) collective-permute-start(f32[4,4,1,256]{3,1,0,2:T(4,128)} %get-tuple-element.40), channel_id=1, source_target_pairs={{1,0},{2,1},{3,2},{4,3},{5,4},{6,5},{7,6},{9,8},{10,9},{11,10},{12... | collective-permute-start | bytes 49160 | tf_op jit(solution)/shard_map/ppermute | solution.py:30
  23.6 30.1 %copy-start = (f32[4,4,64,256]{3,2,1,0:T(8,128)S(1)}, f32[4,4,64,256]{3,2,1,0:T(8,128)}, u32[]{:S(2)}) copy-start(f32[4,4,64,256]{3,2,1,0:T(8,128)} %param.14) | copy-start | bytes 3145732
  26.7 27.1 %copy-start.2 = (f32[4,64,256]{2,0,1:T(4,128)S(1)}, f32[4,64,256]{2,0,1:T(4,128)}, u32[]{:S(2)}) copy-start(f32[4,64,256]{2,0,1:T(4,128)} %copy.92) | copy-start | bytes 786436
  26.7 27.1 %copy-start.4 = (f32[4,64,256]{2,0,1:T(4,128)S(1)}, f32[4,64,256]{2,0,1:T(4,128)}, u32[]{:S(2)}) copy-start(f32[4,64,256]{2,0,1:T(4,128)} %copy.94) | copy-start | bytes 786436
  26.7 27.0 %collective-permute-start.2 = (f32[4,4,64,1]{3,1,0,2:T(4,128)}, f32[4,4,64,1]{3,1,0,2:T(4,128)S(1)}, u32[]{:S(2)}, u32[]{:S(2)}) collective-permute-start(f32[4,4,64,1]{3,1,0,2:T(4,128)} %get-tuple-element.43), channel_id=1, source_target_pairs={{0,8},{8,16},{16,24},{24,0},{1,9},{9,17},{17,25},{25,1},{2,10},{10... | collective-permute-start | bytes 12296 | tf_op jit(solution)/shard_map/ppermute | solution.py:27
  27.6 30.6 %copy-start.6 = (f32[4,64,256]{2,0,1:T(4,128)}, f32[4,64,256]{2,0,1:T(4,128)S(1)}, u32[]{:S(2)}) copy-start(f32[4,64,256]{2,0,1:T(4,128)S(1)} %copy.93) | copy-start | bytes 786436
  27.6 26.2 %collective-permute-start = (f32[4,4,64,1]{3,1,0,2:T(4,128)}, f32[4,4,64,1]{3,1,0,2:T(4,128)S(1)}, u32[]{:S(2)}, u32[]{:S(2)}) collective-permute-start(f32[4,4,64,1]{3,1,0,2:T(4,128)} %get-tuple-element.44), channel_id=1, source_target_pairs={{8,0},{16,8},{24,16},{0,24},{9,1},{17,9},{25,17},{1,25},{10,2},{18... | collective-permute-start | bytes 12296 | tf_op jit(solution)/shard_map/ppermute | solution.py:30
  29.2 23.2 %collective-permute-start.7 = (f32[4,4,256]{2,1,0:T(4,128)}, f32[4,4,256]{2,1,0:T(4,128)S(1)}, u32[]{:S(2)}, u32[]{:S(2)}) collective-permute-start(f32[4,4,256]{2,1,0:T(4,128)} %collective-permute-done.6), channel_id=1, source_target_pairs={{0,8},{8,16},{16,24},{24,0},{1,9},{9,17},{17,25},{25,1},{2,10},{10... | collective-permute-start | bytes 49160 | tf_op jit(solution)/shard_map/ppermute | solution.py:68
  52.3 5.8 %collective-permute-start.8 = (f32[4,4,256]{2,1,0:T(4,128)S(1)}, f32[4,4,256]{2,1,0:T(4,128)S(1)}, u32[]{:S(2)}, u32[]{:S(2)}) collective-permute-start(f32[4,4,256]{2,1,0:T(4,128)S(1)} %collective-permute-done.7), channel_id=1, source_target_pairs={{0,8},{8,16},{16,24},{24,0},{1,9},{9,17},{17,25},{25,1},{2,10},{10... | collective-permute-start | bytes 49160 | tf_op jit(solution)/shard_map/ppermute | solution.py:68
  64.4 35.0 %copy-start.3 = (f32[4,64,256]{2,0,1:T(4,128)S(1)}, f32[4,64,256]{2,0,1:T(4,128)}, u32[]{:S(2)}) copy-start(f32[4,64,256]{2,0,1:T(4,128)} %copy.92) | copy-start | bytes 786436
  64.4 35.0 %copy-start.5 = (f32[4,64,256]{2,0,1:T(4,128)S(1)}, f32[4,64,256]{2,0,1:T(4,128)}, u32[]{:S(2)}) copy-start(f32[4,64,256]{2,0,1:T(4,128)} %copy.94) | copy-start | bytes 786436
  64.5 35.0 %copy-start.7 = (f32[4,64,256]{2,0,1:T(4,128)S(1)}, f32[4,64,256]{2,0,1:T(4,128)}, u32[]{:S(2)}) copy-start(f32[4,64,256]{2,0,1:T(4,128)} %copy-done.6) | copy-start | bytes 786436
  64.5 35.0 %copy-start.9 = (f32[4,64,256]{2,0,1:T(4,128)S(1)}, f32[4,64,256]{2,0,1:T(4,128)}, u32[]{:S(2)}) copy-start(f32[4,64,256]{2,0,1:T(4,128)} %copy-done.8) | copy-start | bytes 786436
  64.5 8.7 %collective-permute-start.13 = (f32[4,4,256]{2,1,0:T(4,128)S(1)}, f32[4,4,256]{2,1,0:T(4,128)S(1)}, u32[]{:S(2)}, u32[]{:S(2)}) collective-permute-start(f32[4,4,256]{2,1,0:T(4,128)S(1)} %bitcast_multiply_fusion.1), channel_id=1, source_target_pairs={{0,8},{8,16},{16,24},{24,0},{1,9},{9,17},{17,25},{25,1},{2,10},{10... | collective-permute-start | bytes 49160 | tf_op jit(solution)/shard_map/ppermute | solution.py:68
  65.1 34.3 %collective-permute-start.12 = (f32[4,4,1,256]{3,1,0,2:T(4,128)S(1)}, f32[4,4,1,256]{3,1,0,2:T(4,128)S(1)}, u32[]{:S(2)}, u32[]{:S(2)}) collective-permute-start(f32[4,4,1,256]{3,1,0,2:T(4,128)S(1)} %get-tuple-element.31), channel_id=1, source_target_pairs={{0,1},{1,2},{2,3},{3,4},{4,5},{5,6},{6,7},{8,9},{9,10},{10,11},{11... | collective-permute-start | bytes 49160 | tf_op jit(solution)/shard_map/ppermute | solution.py:27
  67.0 32.4 %collective-permute-start.11 = (f32[4,4,1,256]{3,1,0,2:T(4,128)S(1)}, f32[4,4,1,256]{3,1,0,2:T(4,128)S(1)}, u32[]{:S(2)}, u32[]{:S(2)}) collective-permute-start(f32[4,4,1,256]{3,1,0,2:T(4,128)S(1)} %get-tuple-element.32), channel_id=1, source_target_pairs={{1,0},{2,1},{3,2},{4,3},{5,4},{6,5},{7,6},{9,8},{10,9},{11,10},{12... | collective-permute-start | bytes 49160 | tf_op jit(solution)/shard_map/ppermute | solution.py:30
  70.7 28.7 %collective-permute-start.10 = (f32[4,4,64,1]{3,1,0,2:T(4,128)S(1)}, f32[4,4,64,1]{3,1,0,2:T(4,128)S(1)}, u32[]{:S(2)}, u32[]{:S(2)}) collective-permute-start(f32[4,4,64,1]{3,1,0,2:T(4,128)S(1)} %get-tuple-element.35), channel_id=1, source_target_pairs={{0,8},{8,16},{16,24},{24,0},{1,9},{9,17},{17,25},{25,1},{2,10},{10... | collective-permute-start | bytes 12296 | tf_op jit(solution)/shard_map/ppermute | solution.py:27
  73.1 26.3 %collective-permute-start.9 = (f32[4,4,64,1]{3,1,0,2:T(4,128)S(1)}, f32[4,4,64,1]{3,1,0,2:T(4,128)S(1)}, u32[]{:S(2)}, u32[]{:S(2)}) collective-permute-start(f32[4,4,64,1]{3,1,0,2:T(4,128)S(1)} %get-tuple-element.36), channel_id=1, source_target_pairs={{8,0},{16,8},{24,16},{0,24},{9,1},{17,9},{25,17},{1,25},{10,2},{18... | collective-permute-start | bytes 12296 | tf_op jit(solution)/shard_map/ppermute | solution.py:30
  73.1 23.0 %collective-permute-start.14 = (f32[4,4,256]{2,1,0:T(4,128)S(1)}, f32[4,4,256]{2,1,0:T(4,128)S(1)}, u32[]{:S(2)}, u32[]{:S(2)}) collective-permute-start(f32[4,4,256]{2,1,0:T(4,128)S(1)} %collective-permute-done.13), channel_id=1, source_target_pairs={{0,8},{8,16},{16,24},{24,0},{1,9},{9,17},{17,25},{25,1},{2,10},{10... | collective-permute-start | bytes 49160 | tf_op jit(solution)/shard_map/ppermute | solution.py:68
  96.1 6.1 %collective-permute-start.15 = (f32[4,4,256]{2,1,0:T(4,128)S(1)}, f32[4,4,256]{2,1,0:T(4,128)S(1)}, u32[]{:S(2)}, u32[]{:S(2)}) collective-permute-start(f32[4,4,256]{2,1,0:T(4,128)S(1)} %collective-permute-done.14), channel_id=1, source_target_pairs={{0,8},{8,16},{16,24},{24,0},{1,9},{9,17},{17,25},{25,1},{2,10},{10... | collective-permute-start | bytes 49160 | tf_op jit(solution)/shard_map/ppermute | solution.py:68
  (10 other events, 134.9 us)
